TPU v7x, 256 devices: a whole 4x4x8 slice. The times are simulated.
256 devices in a mesh: row: 8 (over x, core), col: 16 (over z, y_hi), layer: 2 (over y_lo).
Axes of the slice: x: 4, y: 4 (y_hi: 2, y_lo: 2; y = y_hi * 2 + y_lo), z: 8, core: 2. Of those that a mesh axis runs over, the one named last changes fastest.
Arguments:
- interface_panel: float32 [2048, 1024], P('col', 'row'), may hold values from -6 to 6
- coupling: float32 [2, 2, 2048, 2048], P('layer', None, 'row', 'col'), may hold values from -0.0625 to 0.0625
- solved_coupling: float32 [8192, 1024], P(('layer', 'col'), 'row'), may hold values from -6 to 6
Outputs:
- schur_panel: float32 [2048, 1024], P('col', 'row')
All inputs are finite; a program needn't handle non-finite values.
Results may differ from a plain program's by a relative error of at most 0.00007.
Values sent between devices are 32-bit elements; how exact they have to be, the bound alone decides.
A program may use at most 64 MiB of HBM per device.

v0:
```python
import jax
import jax.numpy as jnp
from jax import lax
from jax.sharding import PartitionSpec as P


def shards(interface_panel, coupling, solved_coupling):
    blocks = coupling[0]
    depth = blocks.shape[0] * blocks.shape[1] * lax.axis_size("row")
    gathered_b = lax.all_gather(blocks, "row", axis=1, tiled=True).reshape(depth, blocks.shape[2])
    gathered_y = lax.all_gather(solved_coupling, "col", axis=0, tiled=True)
    partial = lax.dot_general(
        gathered_b,
        gathered_y,
        (((0,), (0,)), ((), ())),
        precision=lax.Precision.HIGHEST,
        preferred_element_type=jnp.float32,
    )
    other = lax.ppermute(partial, "layer", [(0, 1), (1, 0)])
    return interface_panel - (partial + other)


def solution(mesh):
    return jax.shard_map(
        shards,
        mesh=mesh,
        in_specs=(P("col", "row"), P("layer", None, "row", "col"), P(("layer", "col"), "row")),
        out_specs=P("col", "row"),
        check_vma=False,
    )
```

profile of v0, /device:TPU:2, one launch (start us, length us, event | category | flops | bytes accessed | tf_op | source)
XLA Modules:
  0.0 145.9 jit_solution(16994233739036828383)
XLA Ops:
  6.5 0.0 all-gather.6.cloned.1.call-start
  6.5 0.7 all-gather.6.cloned.1.call-update
  7.3 0.0 all-gather.4.cloned.1.call-start
  7.3 0.7 all-gather.4.cloned.1.call-update
  8.0 31.0 %all-gather.6.cloned.1.call-done = f32[1,2,2048,128]{3,2,1,0:T(8,128)} async-done(((f32[1,2,256,128]{3,2,1,0:T(8,128)}), f32[1,2,2048,128]{3,2,1,0:T(8,128)}) %all-gather.6.cloned.1.call-update) | async-done | bytes 2097168 | tf_op jit(solution)/shard_map/all_gather | solution.py:10
  39.0 89.4 %all-gather.4.cloned.1.call-done = f32[4096,128]{1,0:T(8,128)} async-done(((f32[256,128]{1,0:T(8,128)}), f32[4096,128]{1,0:T(8,128)}) %all-gather.4.cloned.1.call-update) | async-done | bytes 2097168 | tf_op jit(solution)/shard_map/all_gather | solution.py:11
  128.4 0.0 copy-start
  128.4 5.7 %fusion = f32[128,128]{1,0:T(8,128)S(1)} fusion(f32[4096,128]{1,0:T(8,128)} %bitcast.3, f32[4096,128]{1,0:T(8,128)} %all-gather.4.cloned.1.call-done), kind=kOutput, calls=%fused_computation.1 | convolution fusion | flops 805306368 | bytes 4259840 | tf_op jit(solution)/shard_map/dot_general | solution.py:12
  134.1 0.7 collective-permute-start
  134.7 3.7 %collective-permute-done = f32[128,128]{1,0:T(8,128)S(1)} collective-permute-done((f32[128,128]{1,0:T(8,128)S(1)}, f32[128,128]{1,0:T(8,128)S(1)}, u32[]{:S(2)}, u32[]{:S(2)}) %collective-permute-start) | collective-permute-done | bytes 65568 | tf_op jit(solution)/shard_map/ppermute | solution.py:19
  138.4 0.0 copy-done
  138.4 0.6 add_subtract_fusion
Async XLA Ops:
  6.5 32.4 %all-gather.6.cloned.1.call-start = ((), (), s32[]{:S(2)}) async-start(), calls=%async_computation.1 | async-start | bytes 2359296 | tf_op jit(solution)/shard_map/all_gather | solution.py:10
  7.3 121.1 %all-gather.4.cloned.1.call-start = ((), (), s32[]{:S(2)}) async-start(), calls=%async_computation | async-start | bytes 2228224 | tf_op jit(solution)/shard_map/all_gather | solution.py:11
  128.4 10.1 %copy-start = (f32[128,128]{1,0:T(8,128)S(1)}, f32[128,128]{1,0:T(8,128)}, u32[]{:S(2)}) copy-start(f32[128,128]{1,0:T(8,128)} %param.3) | copy-start | bytes 196612
  134.1 4.4 %collective-permute-start = (f32[128,128]{1,0:T(8,128)S(1)}, f32[128,128]{1,0:T(8,128)S(1)}, u32[]{:S(2)}, u32[]{:S(2)}) collective-permute-start(f32[128,128]{1,0:T(8,128)S(1)} %fusion), channel_id=1, source_target_pairs={{0,1},{1,0},{2,3},{3,2},{4,5},{5,4},{6,7},{7,6},{8,9},{9,8},{10,11... | collective-permute-start | bytes 196616 | tf_op jit(solution)/shard_map/ppermute | solution.py:19
Sparse Core Ops, SparseCore 0:
  9.2 29.7 all-gather.5
  41.6 86.7 all-gather.3
where the time goes:
time: 146 us
  waiting for transfers between devices  125 us (86%)
  between operations  13.4 us (9%)
  matrix products  5.7 us (4%)
    all_gather x1, waiting for transfers between devices, shards(): gathered_y = lax.all_gather(solved_coupling, 'col', axis=0, tiled=True)  89.4 us
    all_gather x1, waiting for transfers between devices, shards(): lax.all_gather(blocks, 'row', axis=1, tiled=True)  31 us
    dot_general x1, matrix products, shards(): lax.dot_general(gathered_b, gathered_y, (((0,), (0,)), ((), ())), precisi...  5.7 us
    ppermute x1, waiting for transfers between devices, shards(): other = lax.ppermute(partial, 'layer', [(0, 1), (1, 0)])  3.68 us
  transfers between devices with their start and end apart: 3, of which 3 were waited for; matrix products, arithmetic and copies ran while one was open for 0% of the time, Pallas kernels for 0%

commit v1 on v0

--- a/solution.py
+++ b/solution.py
@@ -4,10 +4,23 @@
 from jax.sharding import PartitionSpec as P
 
 
+def ring_gather(x, axis, dim):
+    ways = lax.axis_size(axis)
+    up = [(d, (d + 1) % ways) for d in range(ways)]
+    down = [(d, (d - 1) % ways) for d in range(ways)]
+    earlier, later = ([x], [x])
+    for _ in range(ways // 2):
+        earlier.append(lax.ppermute(earlier[-1], axis, up))
+    for _ in range((ways - 1) // 2):
+        later.append(lax.ppermute(later[-1], axis, down))
+    line = jnp.concatenate([*earlier[::-1], *later[1:]], axis=dim)
+    return jnp.roll(line, (lax.axis_index(axis) - ways // 2) * x.shape[dim], axis=dim)
+
+
 def shards(interface_panel, coupling, solved_coupling):
     blocks = coupling[0]
     depth = blocks.shape[0] * blocks.shape[1] * lax.axis_size("row")
-    gathered_b = lax.all_gather(blocks, "row", axis=1, tiled=True).reshape(depth, blocks.shape[2])
+    gathered_b = ring_gather(blocks, "row", 1).reshape(depth, blocks.shape[2])
     gathered_y = lax.all_gather(solved_coupling, "col", axis=0, tiled=True)
     partial = lax.dot_general(
         gathered_b,

time: 146 us -> 116 us (0.79)
  waiting for transfers between devices: 125 us -> 88.3 us
  starting transfers between devices: 0.71 us -> 6.44 us
    all_gather x1 -> x0, waiting for transfers between devices: 31 us -> none  [shards(): lax.all_gather(blocks, 'row', axis=1, tiled=True)]
    all_gather x1, waiting for transfers between devices: 89.4 us -> 66.3 us  [shards(): gathered_y = lax.all_gather(solved_coupling, 'col', axis=0, tiled=True)]
    ppermute x0 -> x7, waiting for transfers between devices: none -> 17.6 us  [the longest x4 17.1 us: ring_gather(): earlier.append(lax.ppermute(earlier[-1], axis, up))]
    ppermute x0 -> x7, starting transfers between devices: none -> 5.77 us  [the longest x3 5.75 us: ring_gather(): later.append(lax.ppermute(later[-1], axis, down))]
  transfers between devices with their start and end apart: 3 -> 9, of which waited for: 3 -> 8; matrix products, arithmetic and copies ran while one was open for 0% -> 1% of each run, Pallas kernels for 0% -> 0%
where the time goes in v1:
time: 116 us; the launch traced here: 115 us
  waiting for transfers between devices  88.3 us (76%)
  between operations  13.6 us (12%)
  starting transfers between devices  6.44 us (6%)
  matrix products  5.03 us (4%)
  local copies, waits for them, and re-layouts  1.42 us (1%)
    all_gather x1, waiting for transfers between devices, shards(): gathered_y = lax.all_gather(solved_coupling, 'col', axis=0, tiled=True)  66.3 us
    ppermute x4, waiting for transfers between devices, ring_gather(): earlier.append(lax.ppermute(earlier[-1], axis, up))  17.1 us
    ppermute x3, starting transfers between devices, ring_gather(): later.append(lax.ppermute(later[-1], axis, down))  5.75 us
    dot_general x1, matrix products, shards(): lax.dot_general(gathered_b, gathered_y, (((0,), (0,)), ((), ())), precisi...  5.03 us
    ppermute x1, waiting for transfers between devices, shards(): other = lax.ppermute(partial, 'layer', [(0, 1), (1, 0)])  3.68 us
  transfers between devices with their start and end apart: 9, of which 8 were waited for; matrix products, arithmetic and copies ran while one was open for 1% of the time, Pallas kernels for 0%

profile of v1, /device:TPU:2, one launch (start us, length us, event | category | flops | bytes accessed | tf_op | source)
XLA Modules:
  0.0 115.4 jit_solution(965974663749398955)
XLA Ops:
  6.5 0.0 all-gather.2.cloned.1.call-start
  6.5 0.7 all-gather.2.cloned.1.call-update
  7.3 0.0 collective-permute-start
  7.3 6.0 %collective-permute-done = f32[2,256,128]{2,1,0:T(8,128)S(1)} collective-permute-done((f32[2,256,128]{2,1,0:T(8,128)}, f32[2,256,128]{2,1,0:T(8,128)S(1)}, u32[]{:S(2)}, u32[]{:S(2)}) %collective-permute-start) | collective-permute-done | bytes 262176 | tf_op jit(solution)/shard_map/ppermute | solution.py:13
  13.3 0.0 collective-permute-start.1
  13.3 1.7 %collective-permute-start.4 = (f32[2,256,128]{2,1,0:T(8,128)}, f32[2,256,128]{2,1,0:T(8,128)S(1)}, u32[]{:S(2)}, u32[]{:S(2)}) collective-permute-start(f32[2,256,128]{2,1,0:T(8,128)} %bitcast.8), channel_id=1, source_target_pairs={{0,224},{32,0},{64,32},{96,64},{128,96},{160,128},{192,160},{224,1... | collective-permute-start | bytes 786440 | tf_op jit(solution)/shard_map/ppermute | solution.py:15
  15.0 4.1 %collective-permute-done.1 = f32[2,256,128]{2,1,0:T(8,128)S(1)} collective-permute-done((f32[2,256,128]{2,1,0:T(8,128)S(1)}, f32[2,256,128]{2,1,0:T(8,128)S(1)}, u32[]{:S(2)}, u32[]{:S(2)}) %collective-permute-start.1) | collective-permute-done | bytes 262176 | tf_op jit(solution)/shard_map/ppermute | solution.py:13
  19.1 0.0 collective-permute-start.2
  19.1 0.2 collective-permute-done.4
  19.2 2.1 %collective-permute-start.5 = (f32[2,256,128]{2,1,0:T(8,128)S(1)}, f32[2,256,128]{2,1,0:T(8,128)S(1)}, u32[]{:S(2)}, u32[]{:S(2)}) collective-permute-start(f32[2,256,128]{2,1,0:T(8,128)S(1)} %collective-permute-done.4), channel_id=1, source_target_pairs={{0,224},{32,0},{64,32},{96,64},{128,96},{160,128},{192,160},{224,1... | collective-permute-start | bytes 786440 | tf_op jit(solution)/shard_map/ppermute | solution.py:15
  21.3 3.5 %collective-permute-done.2 = f32[2,256,128]{2,1,0:T(8,128)S(1)} collective-permute-done((f32[2,256,128]{2,1,0:T(8,128)S(1)}, f32[2,256,128]{2,1,0:T(8,128)S(1)}, u32[]{:S(2)}, u32[]{:S(2)}) %collective-permute-start.2) | collective-permute-done | bytes 262176 | tf_op jit(solution)/shard_map/ppermute | solution.py:13
  24.9 0.0 collective-permute-start.3
  24.9 0.3 collective-permute-done.5
  25.2 1.9 %collective-permute-start.6 = (f32[2,256,128]{2,1,0:T(8,128)S(1)}, f32[2,256,128]{2,1,0:T(8,128)S(1)}, u32[]{:S(2)}, u32[]{:S(2)}) collective-permute-start(f32[2,256,128]{2,1,0:T(8,128)S(1)} %collective-permute-done.5), channel_id=1, source_target_pairs={{0,224},{32,0},{64,32},{96,64},{128,96},{160,128},{192,160},{224,1... | collective-permute-start | bytes 786440 | tf_op jit(solution)/shard_map/ppermute | solution.py:15
  27.1 3.5 %collective-permute-done.3 = f32[2,256,128]{2,1,0:T(8,128)S(1)} collective-permute-done((f32[2,256,128]{2,1,0:T(8,128)S(1)}, f32[2,256,128]{2,1,0:T(8,128)S(1)}, u32[]{:S(2)}, u32[]{:S(2)}) %collective-permute-start.3) | collective-permute-done | bytes 262176 | tf_op jit(solution)/shard_map/ppermute | solution.py:13
  30.8 1.0 constant_dynamic-update-slice_fusion.11
  31.8 0.0 collective-permute-done.6
  32.1 0.0 copy-start.1
  32.1 0.1 constant_dynamic-slice_fusion
  32.2 66.3 %all-gather.2.cloned.1.call-done = f32[4096,128]{1,0:T(8,128)} async-done(((f32[256,128]{1,0:T(8,128)}), f32[4096,128]{1,0:T(8,128)}) %all-gather.2.cloned.1.call-update) | async-done | bytes 2097168 | tf_op jit(solution)/shard_map/all_gather | solution.py:24
  98.5 5.0 %fusion = f32[128,128]{1,0:T(8,128)S(1)} fusion(f32[4096,128]{1,0:T(8,128)S(1)} %bitcast.6, f32[4096,128]{1,0:T(8,128)} %all-gather.2.cloned.1.call-done), kind=kOutput, calls=%fused_computation.18 | convolution fusion | flops 805306368 | bytes 4259840 | tf_op jit(solution)/shard_map/dot_general | solution.py:25
  103.6 0.7 collective-permute-start.7
  104.2 3.7 %collective-permute-done.7 = f32[128,128]{1,0:T(8,128)S(1)} collective-permute-done((f32[128,128]{1,0:T(8,128)S(1)}, f32[128,128]{1,0:T(8,128)S(1)}, u32[]{:S(2)}, u32[]{:S(2)}) %collective-permute-start.7) | collective-permute-done | bytes 65568 | tf_op jit(solution)/shard_map/ppermute | solution.py:32
  107.9 0.6 add_subtract_fusion
  (18 shorter events, 0.3 us)
Async XLA Ops:
  6.5 25.4 %copy-start = (f32[1,2,256,128]{3,2,1,0:T(8,128)S(1)}, f32[1,2,256,128]{3,2,1,0:T(8,128)}, u32[]{:S(2)}) copy-start(f32[1,2,256,128]{3,2,1,0:T(8,128)} %param.4) | copy-start | bytes 786436
  6.5 92.0 %all-gather.2.cloned.1.call-start = ((), (), s32[]{:S(2)}) async-start(), calls=%async_computation | async-start | bytes 2228224 | tf_op jit(solution)/shard_map/all_gather | solution.py:24
  7.3 6.0 %collective-permute-start = (f32[2,256,128]{2,1,0:T(8,128)}, f32[2,256,128]{2,1,0:T(8,128)S(1)}, u32[]{:S(2)}, u32[]{:S(2)}) collective-permute-start(f32[2,256,128]{2,1,0:T(8,128)} %bitcast.7), channel_id=1, source_target_pairs={{0,32},{32,64},{64,96},{96,128},{128,160},{160,192},{192,224},{224... | collective-permute-start | bytes 786440 | tf_op jit(solution)/shard_map/ppermute | solution.py:13
  13.3 5.8 %collective-permute-start.1 = (f32[2,256,128]{2,1,0:T(8,128)S(1)}, f32[2,256,128]{2,1,0:T(8,128)S(1)}, u32[]{:S(2)}, u32[]{:S(2)}) collective-permute-start(f32[2,256,128]{2,1,0:T(8,128)S(1)} %collective-permute-done), channel_id=1, source_target_pairs={{0,32},{32,64},{64,96},{96,128},{128,160},{160,192},{192,224},{224... | collective-permute-start | bytes 786440 | tf_op jit(solution)/shard_map/ppermute | solution.py:13
  13.3 6.0 %collective-permute-start.4 = (f32[2,256,128]{2,1,0:T(8,128)}, f32[2,256,128]{2,1,0:T(8,128)S(1)}, u32[]{:S(2)}, u32[]{:S(2)}) collective-permute-start(f32[2,256,128]{2,1,0:T(8,128)} %bitcast.8), channel_id=1, source_target_pairs={{0,224},{32,0},{64,32},{96,64},{128,96},{160,128},{192,160},{224,1... | collective-permute-start | bytes 786440 | tf_op jit(solution)/shard_map/ppermute | solution.py:15
  19.1 5.8 %collective-permute-start.2 = (f32[2,256,128]{2,1,0:T(8,128)S(1)}, f32[2,256,128]{2,1,0:T(8,128)S(1)}, u32[]{:S(2)}, u32[]{:S(2)}) collective-permute-start(f32[2,256,128]{2,1,0:T(8,128)S(1)} %collective-permute-done.1), channel_id=1, source_target_pairs={{0,32},{32,64},{64,96},{96,128},{128,160},{160,192},{192,224},{224... | collective-permute-start | bytes 786440 | tf_op jit(solution)/shard_map/ppermute | solution.py:13
  19.2 6.0 %collective-permute-start.5 = (f32[2,256,128]{2,1,0:T(8,128)S(1)}, f32[2,256,128]{2,1,0:T(8,128)S(1)}, u32[]{:S(2)}, u32[]{:S(2)}) collective-permute-start(f32[2,256,128]{2,1,0:T(8,128)S(1)} %collective-permute-done.4), channel_id=1, source_target_pairs={{0,224},{32,0},{64,32},{96,64},{128,96},{160,128},{192,160},{224,1... | collective-permute-start | bytes 786440 | tf_op jit(solution)/shard_map/ppermute | solution.py:15
  24.9 5.8 %collective-permute-start.3 = (f32[2,256,128]{2,1,0:T(8,128)S(1)}, f32[2,256,128]{2,1,0:T(8,128)S(1)}, u32[]{:S(2)}, u32[]{:S(2)}) collective-permute-start(f32[2,256,128]{2,1,0:T(8,128)S(1)} %collective-permute-done.2), channel_id=1, source_target_pairs={{0,32},{32,64},{64,96},{96,128},{128,160},{160,192},{192,224},{224... | collective-permute-start | bytes 786440 | tf_op jit(solution)/shard_map/ppermute | solution.py:13
  25.2 6.6 %collective-permute-start.6 = (f32[2,256,128]{2,1,0:T(8,128)S(1)}, f32[2,256,128]{2,1,0:T(8,128)S(1)}, u32[]{:S(2)}, u32[]{:S(2)}) collective-permute-start(f32[2,256,128]{2,1,0:T(8,128)S(1)} %collective-permute-done.5), channel_id=1, source_target_pairs={{0,224},{32,0},{64,32},{96,64},{128,96},{160,128},{192,160},{224,1... | collective-permute-start | bytes 786440 | tf_op jit(solution)/shard_map/ppermute | solution.py:15
  32.1 75.9 %copy-start.1 = (f32[128,128]{1,0:T(8,128)S(1)}, f32[128,128]{1,0:T(8,128)}, u32[]{:S(2)}) copy-start(f32[128,128]{1,0:T(8,128)} %param.3) | copy-start | bytes 196612
  103.6 4.4 %collective-permute-start.7 = (f32[128,128]{1,0:T(8,128)S(1)}, f32[128,128]{1,0:T(8,128)S(1)}, u32[]{:S(2)}, u32[]{:S(2)}) collective-permute-start(f32[128,128]{1,0:T(8,128)S(1)} %fusion), channel_id=1, source_target_pairs={{0,1},{1,0},{2,3},{3,2},{4,5},{5,4},{6,7},{7,6},{8,9},{9,8},{10,11... | collective-permute-start | bytes 196616 | tf_op jit(solution)/shard_map/ppermute | solution.py:32
Sparse Core Ops, SparseCore 0:
  9.9 88.5 all-gather.1
